TPU v7x, 256 devices: a whole 4x4x8 slice. The times are simulated.
256 devices in a mesh: gx: 32 (over z, y_hi, core), gy: 8 (over x, y_lo).
Axes of the slice: x: 4, y: 4 (y_hi: 2, y_lo: 2; y = y_hi * 2 + y_lo), z: 8, core: 2. Of those that a mesh axis runs over, the one named last changes fastest.
Arguments:
- prior_members: float32 [64, 3, 2, 256, 1024], P(None, None, None, 'gx', 'gy'), may hold values from -0.25 to 0.25
- obs_column: int32 [32, 8, 256], P('gx', 'gy'), may hold values from 0 to 1023
- obs_value: float32 [32, 8, 256], P('gx', 'gy'), may hold values from -0.3 to 0.3
- obs_precision: float32 [32, 8, 256], P('gx', 'gy'), may hold values from 20 to 400
- obs_list: int32 [32, 128, 128], P('gx', 'gy'), may hold values from 0 to 2303, as said below
- patch_count: int32 [32, 128], P('gx', 'gy'), may hold values from 1 to 128, as said below
Outputs:
- analysis: float32 [64, 3, 2, 256, 1024], P(None, None, None, 'gx', 'gy')
Inputs may be any that keep to these rules, and one draw needn't show every extreme that they name: `obs_list`: entry e of a patch's list names slot e % 256 of the tile displaced by (e // 256 // 3 - 1, e // 256 % 3 - 1) tiles in (longitude, latitude) from the patch's own tile, longitude wrapping around; never a tile beyond the latitude edges. Entries at and past the patch's count are ignored. `patch_count`: counts differ strongly from tile to tile.
All inputs are finite; a program needn't handle non-finite values.
Results may differ from a plain program's by a relative error of at most 0.0003.
Values sent between devices are 32-bit elements; how exact they have to be, the bound alone decides.
No kernel may reach another device: no remote copies, remote signals or barrier semaphores. Data moves between devices by JAX's collectives and lax.ppermute only.
A program may use at most 64 MiB of HBM per device.

v0:
```python
import jax
import jax.numpy as jnp
from jax import lax
from jax.sharding import PartitionSpec as P

CX = 8
CY = 128
TILE_WIDTH_CELLS = 8
STEPS = 3
NS_ITERS = 3


courant = 0.3
highest = lax.Precision.HIGHEST


def padded_2(x, sides, width):
    edges = {}
    for axis, dim in sides:
        devices, length = (lax.axis_size(axis), x.shape[dim])
        up = [(i, (i + 1) % devices) for i in range(devices)]
        last = lax.slice_in_dim(x, length - width, length, axis=dim)
        initial = lax.slice_in_dim(x, 0, width, axis=dim)
        edges[dim] = (
            lax.ppermute(last, axis, up),
            lax.ppermute(initial, axis, [(b, a) for a, b in up]),
        )
    done = []
    for _, dim in sides:
        low, high = edges[dim]
        around = [(width, width) if d in done else (0, 0) for d in range(x.ndim)]
        x = jnp.concatenate([jnp.pad(low, around), x, jnp.pad(high, around)], axis=dim)
        done.append(dim)
    return x


def padded_3(x, sides, width):
    for axis, dim in sides:
        devices, length = (lax.axis_size(axis), x.shape[dim])
        up = [(i, (i + 1) % devices) for i in range(devices)]
        down = [(j, i) for i, j in up]
        last = lax.slice_in_dim(x, length - width, length, axis=dim)
        initial = lax.slice_in_dim(x, 0, width, axis=dim)
        before = lax.ppermute(last, axis, up)
        after = lax.ppermute(initial, axis, down)
        x = jnp.concatenate([before, x, after], axis=dim)
    return x


def friedrichs_step(padded):
    depths = 1.0 + padded[..., 0, :, :, :]
    momentum_x = padded[..., 1, :, :, :]
    momentum_y = padded[..., 2, :, :, :]
    pressure = 0.5 * depths * depths
    cross_flux = momentum_x * momentum_y / depths
    flux_x = jnp.stack(
        [momentum_x, momentum_x * momentum_x / depths + pressure, cross_flux], axis=-4
    )
    flux_y = jnp.stack(
        [momentum_y, cross_flux, momentum_y * momentum_y / depths + pressure], axis=-4
    )
    neighbours = (
        padded[..., 2:, 1:-1]
        + padded[..., :-2, 1:-1]
        + padded[..., 1:-1, 2:]
        + padded[..., 1:-1, :-2]
    )
    return (
        0.25 * neighbours
        - 0.5 * courant * (flux_x[..., 2:, 1:-1] - flux_x[..., :-2, 1:-1])
        - 0.5 * courant * (flux_y[..., 1:-1, 2:] - flux_y[..., 1:-1, :-2])
    )


def cut_outside(padded, patch_border):
    extent = padded.shape[-1] - 2 * patch_border
    global_rows = (
        lax.iota(jnp.int32, padded.shape[-1]) + lax.axis_index("gy") * extent - patch_border
    )
    inside = (global_rows >= 0) & (global_rows < extent * lax.axis_size("gy"))
    return padded * inside.astype(padded.dtype)


def analyse(fields, members_obs, values, precisions, offset_x, offset_y, usable):
    members = fields.shape[1]
    obs_mean = jnp.mean(members_obs, axis=1)
    obs_pert = members_obs - obs_mean[:, None, :]
    departure = values - obs_mean
    weights = usable * precisions * jnp.exp(-((offset_x / CX) ** 2) - (offset_y / CY) ** 2)
    gram_matrix = jnp.einsum(
        "bkm,bjm->bkj", obs_pert * weights[:, None, :], obs_pert, precision=highest
    )
    bounds = members - 1.0 + jnp.sum(weights * jnp.sum(obs_pert * obs_pert, axis=1), axis=1)
    identity = jnp.eye(members, dtype=jnp.float32)
    scaled = (gram_matrix + (members - 1.0) * identity) / bounds[:, None, None]
    iterate = scaled
    inverse_root = jnp.broadcast_to(identity, scaled.shape)
    for repeat in range(NS_ITERS):
        factor = 1.5 * identity - 0.5 * jnp.einsum(
            "bij,bjk->bik", inverse_root, iterate, precision=highest
        )
        iterate = jnp.einsum("bij,bjk->bik", iterate, factor, precision=highest)
        inverse_root = jnp.einsum("bij,bjk->bik", factor, inverse_root, precision=highest)
    forcing = jnp.einsum("bkm,bm->bk", obs_pert, weights * departure, precision=highest)
    half_way = jnp.einsum("bij,bj->bi", inverse_root, forcing, precision=highest)
    mean_weight = (
        jnp.einsum("bij,bj->bi", inverse_root, half_way, precision=highest) / bounds[:, None]
    )
    spread_weight = jnp.sqrt((members - 1.0) / bounds)[:, None, None] * inverse_root
    combined = spread_weight + mean_weight[:, :, None]
    field_mean = jnp.mean(fields, axis=1)
    field_pert = fields - field_mean[:, None, :]
    return field_mean[:, None, :] + jnp.einsum(
        "bif,bik->bkf", field_pert, combined, precision=highest
    )


def local(prior_members, obs_column, obs_value, obs_precision, obs_list, patch_count):
    members = prior_members.shape[0]
    levels = prior_members.shape[2]
    width_x = prior_members.shape[3]
    width_y = prior_members.shape[4]
    states = prior_members
    for repeat in range(STEPS):
        padded = padded_2(states, (("gx", 3), ("gy", 4)), 1)
        states = friedrichs_step(cut_outside(padded, 1))
    layer_mean_value = jnp.mean(states[:, 0], axis=1).reshape(members, width_x * width_y)
    columns = obs_column[0, 0]
    members_obs = jnp.take(layer_mean_value, columns, axis=1)
    local_x = (columns // width_y).astype(jnp.float32)
    local_y = (columns % width_y).astype(jnp.float32)
    extras = jnp.stack([obs_value[0, 0], obs_precision[0, 0], local_x, local_y], axis=0)
    obs_info = jnp.concatenate([members_obs, extras], axis=0)[None, None]
    beside_all = padded_3(obs_info, (("gx", 0), ("gy", 1)), 1)
    info_rows = beside_all.shape[2]
    slot_total = beside_all.shape[3]
    obs_table = jnp.transpose(beside_all, (2, 0, 1, 3)).reshape(info_rows, 9 * slot_total)
    patches_x = width_x // TILE_WIDTH_CELLS
    patches_y = width_y // TILE_WIDTH_CELLS
    batch = patches_x * patches_y
    capacity = obs_list.shape[2]
    entries = obs_list.reshape(batch, capacity)
    offset = entries // slot_total
    shift_x = offset // 3 - 1
    shift_y = offset % 3 - 1
    picked = jnp.take(obs_table, entries.reshape(-1), axis=1).reshape(info_rows, batch, capacity)
    picked_obs = jnp.transpose(picked[:members], (1, 0, 2))
    patch_x = jnp.repeat(jnp.arange(patches_x, dtype=jnp.int32), patches_y)
    patch_y = jnp.tile(jnp.arange(patches_y, dtype=jnp.int32), patches_x)
    centre_x = (patch_x * TILE_WIDTH_CELLS).astype(jnp.float32) + (TILE_WIDTH_CELLS - 1) * 0.5
    centre_y = (patch_y * TILE_WIDTH_CELLS).astype(jnp.float32) + (TILE_WIDTH_CELLS - 1) * 0.5
    offset_x = (shift_x * CX).astype(jnp.float32) + picked[members + 2] - centre_x[:, None]
    offset_y = (shift_y * CY).astype(jnp.float32) + picked[members + 3] - centre_y[:, None]
    slot_range = jnp.arange(capacity, dtype=jnp.int32)
    usable = (slot_range[None, :] < patch_count.reshape(batch)[:, None]).astype(jnp.float32)
    blocks = states.reshape(
        members, 3, levels, patches_x, TILE_WIDTH_CELLS, patches_y, TILE_WIDTH_CELLS
    )
    fields = jnp.transpose(blocks, (3, 5, 0, 1, 2, 4, 6)).reshape(
        batch, members, 3 * levels * TILE_WIDTH_CELLS * TILE_WIDTH_CELLS
    )
    result = analyse(
        fields, picked_obs, picked[members], picked[members + 1], offset_x, offset_y, usable
    )
    result = result.reshape(
        patches_x, patches_y, members, 3, levels, TILE_WIDTH_CELLS, TILE_WIDTH_CELLS
    )
    return jnp.transpose(result, (2, 3, 4, 0, 5, 1, 6)).reshape(
        members, 3, levels, width_x, width_y
    )


def solution(mesh):
    return jax.shard_map(
        local,
        mesh=mesh,
        in_specs=(
            P(None, None, None, "gx", "gy"),
            P("gx", "gy", None),
            P("gx", "gy", None),
            P("gx", "gy", None),
            P("gx", "gy", None),
            P("gx", "gy"),
        ),
        out_specs=P(None, None, None, "gx", "gy"),
        check_vma=False,
    )
```

profile of v0, /device:TPU:2, one launch (start us, length us, event | category | flops | bytes accessed | tf_op | source)
XLA Modules:
  0.0 135.3 jit_solution(8409437406026732640)
XLA Ops:
  0.0 2.1 %copy.50 = f32[64,3,2,8,128]{0,4,3,2,1:T(8,128)S(1)} copy(f32[64,3,2,8,128]{4,3,2,1,0:T(8,128)} %param.6) | data formatting | bytes 3145728 | tf_op args[0]
  2.1 0.9 fusion.78
  3.1 7.9 %collective-permute-start.2 = (f32[64,3,2,1,128]{0,4,3,2,1:T(8,128)}, f32[64,3,2,1,128]{0,4,3,2,1:T(8,128)}, u32[]{:S(2)}, u32[]{:S(2)}) collective-permute-start(f32[64,3,2,1,128]{0,4,3,2,1:T(8,128)} %get-tuple-element.37), channel_id=1, source_target_pairs={{8,0},{16,8},{24,16},{32,24},{40,32},{48,40},{56,48},{64,56},{72,6... | collective-permute-start | bytes 589832 | tf_op jit(solution)/shard_map/ppermute | solution.py:26
  11.1 0.8 collective-permute-start
  11.8 2.2 %collective-permute-start.3 = (f32[64,3,2,8,1]{0,4,3,2,1:T(1,128)S(1)}, f32[64,3,2,8,1]{0,4,3,2,1:T(1,128)S(1)}, u32[]{:S(2)}, u32[]{:S(2)}) collective-permute-start(f32[64,3,2,8,1]{0,4,3,2,1:T(1,128)S(1)} %get-tuple-element.39), channel_id=1, source_target_pairs={{1,0},{2,1},{3,2},{4,3},{5,4},{6,5},{7,6},{0,7},{9,8},{10,9},{11,1... | collective-permute-start | bytes 36872 | tf_op jit(solution)/shard_map/ppermute | solution.py:26
  14.1 0.6 fusion.43
  16.0 0.8 fusion.40
  18.0 1.8 %fusion.2 = f32[64,3,2,10,130]{0,4,3,2,1:T(8,128)S(1)} fusion(f32[64,3,2,8,1]{0,4,3,2,1:T(1,128)S(1)} %collective-permute-done.3, f32[64,3,2,8,1]{0,4,3,2,1:T(1,128)S(1)} %collective-permute-done, f32[64,3,2,1,128]{0,4,3,2,1:T(8,128)} %collective-permute-done.2, f32[64,3,2,8,128]{0,4,3,2,1:T(8,128)S(1)} %copy.50, ...), kind=kLoop, calls=%fused_computation.9 | loop fusion | flops 4492800 | bytes 3987976 | tf_op jit(solution)/shard_map/mul | solution.py:81
  19.9 0.6 fusion.73
  20.5 0.6 pad_maximum_fusion
  21.2 3.1 %fusion.14 = f32[64,3,2,8,128]{0,4,3,2,1:T(8,128)S(1)} fusion(f32[64,3,2,10,130]{0,4,3,2,1:T(8,128)S(1)} %get-tuple-element.45, f32[64,3,2,10,130]{0,4,3,2,1:T(8,128)S(1)} %get-tuple-element.44, f32[64,3,2,10,130]{0,4,3,2,1:T(8,128)S(1)} %fusion.2), kind=kLoop, calls=%fused_computation.41 | loop fusion | flops 3932160 | bytes 14155776 | tf_op jit(solution)/shard_map/sub | solution.py:69
  24.3 2.2 %collective-permute-start.5 = (f32[64,3,2,1,128]{0,4,3,2,1:T(8,128)S(1)}, f32[64,3,2,1,128]{0,4,3,2,1:T(8,128)S(1)}, u32[]{:S(2)}, u32[]{:S(2)}) collective-permute-start(f32[64,3,2,1,128]{0,4,3,2,1:T(8,128)S(1)} %get-tuple-element.32), channel_id=1, source_target_pairs={{0,8},{8,16},{16,24},{24,32},{32,40},{40,48},{48,56},{56,64},{64,7... | collective-permute-start | bytes 589832 | tf_op jit(solution)/shard_map/ppermute | solution.py:25
  26.5 3.3 %collective-permute-start.6 = (f32[64,3,2,1,128]{0,4,3,2,1:T(8,128)S(1)}, f32[64,3,2,1,128]{0,4,3,2,1:T(8,128)S(1)}, u32[]{:S(2)}, u32[]{:S(2)}) collective-permute-start(f32[64,3,2,1,128]{0,4,3,2,1:T(8,128)S(1)} %get-tuple-element.33), channel_id=1, source_target_pairs={{8,0},{16,8},{24,16},{32,24},{40,32},{48,40},{56,48},{64,56},{72,6... | collective-permute-start | bytes 589832 | tf_op jit(solution)/shard_map/ppermute | solution.py:26
  29.8 1.0 collective-permute-start.4
  30.8 2.0 %collective-permute-start.7 = (f32[64,3,2,8,1]{0,4,3,2,1:T(1,128)S(1)}, f32[64,3,2,8,1]{0,4,3,2,1:T(1,128)S(1)}, u32[]{:S(2)}, u32[]{:S(2)}) collective-permute-start(f32[64,3,2,8,1]{0,4,3,2,1:T(1,128)S(1)} %get-tuple-element.35), channel_id=1, source_target_pairs={{1,0},{2,1},{3,2},{4,3},{5,4},{6,5},{7,6},{0,7},{9,8},{10,9},{11,1... | collective-permute-start | bytes 36872 | tf_op jit(solution)/shard_map/ppermute | solution.py:26
  33.4 1.5 %collective-permute-done.4 = f32[64,3,2,8,1]{0,4,3,2,1:T(1,128)S(1)} collective-permute-done((f32[64,3,2,8,1]{0,4,3,2,1:T(1,128)S(1)}, f32[64,3,2,8,1]{0,4,3,2,1:T(1,128)S(1)}, u32[]{:S(2)}, u32[]{:S(2)}) %collective-permute-start.4) | collective-permute-done | bytes 12320 | tf_op jit(solution)/shard_map/ppermute | solution.py:25
  34.9 1.6 %collective-permute-done.7 = f32[64,3,2,8,1]{0,4,3,2,1:T(1,128)S(1)} collective-permute-done((f32[64,3,2,8,1]{0,4,3,2,1:T(1,128)S(1)}, f32[64,3,2,8,1]{0,4,3,2,1:T(1,128)S(1)}, u32[]{:S(2)}, u32[]{:S(2)}) %collective-permute-start.7) | collective-permute-done | bytes 12320 | tf_op jit(solution)/shard_map/ppermute | solution.py:26
  36.5 0.8 fusion.1
  37.3 0.6 fusion.72
  38.0 0.6 pad_maximum_fusion.2
  38.6 3.1 %fusion.9 = f32[64,3,2,8,128]{0,4,3,2,1:T(8,128)S(1)} fusion(f32[64,3,2,10,130]{0,4,3,2,1:T(8,128)S(1)} %get-tuple-element.43, f32[64,3,2,10,130]{0,4,3,2,1:T(8,128)S(1)} %get-tuple-element.42, f32[64,3,2,10,130]{0,4,3,2,1:T(8,128)S(1)} %fusion.1), kind=kLoop, calls=%fused_computation.31 | loop fusion | flops 3932160 | bytes 14155776 | tf_op jit(solution)/shard_map/sub | solution.py:69
  41.7 0.9 fusion.74
  42.7 4.7 %collective-permute-start.10 = (f32[64,3,2,1,128]{0,4,3,2,1:T(8,128)}, f32[64,3,2,1,128]{0,4,3,2,1:T(8,128)S(1)}, u32[]{:S(2)}, u32[]{:S(2)}) collective-permute-start(f32[64,3,2,1,128]{0,4,3,2,1:T(8,128)} %get-tuple-element.29), channel_id=1, source_target_pairs={{8,0},{16,8},{24,16},{32,24},{40,32},{48,40},{56,48},{64,56},{72,6... | collective-permute-start | bytes 589832 | tf_op jit(solution)/shard_map/ppermute | solution.py:26
  47.4 0.7 fusion.75
  48.0 0.8 collective-permute-start.11
  48.9 1.2 collective-permute-start.8
  50.6 1.5 %copy.61 = f32[1,256]{0,1:T(8,128)} copy(f32[1,256]{1,0:T(1,128)} %bitcast.135) | data formatting | bytes 2048 | tf_op jit(solution)/shard_map/stack;squeeze | solution.py:132
  52.1 1.5 %copy.62 = f32[1,256]{0,1:T(8,128)} copy(f32[1,256]{1,0:T(1,128)} %bitcast.136) | data formatting | bytes 2048 | tf_op jit(solution)/shard_map/stack;squeeze | solution.py:132
  54.0 4.7 %collective-permute-done.9 = f32[64,3,2,1,128]{0,4,3,2,1:T(8,128)} collective-permute-done((f32[64,3,2,1,128]{0,4,3,2,1:T(8,128)}, f32[64,3,2,1,128]{0,4,3,2,1:T(8,128)}, u32[]{:S(2)}, u32[]{:S(2)}) %collective-permute-start.9) | collective-permute-done | bytes 196640 | tf_op jit(solution)/shard_map/ppermute | solution.py:25
  58.7 1.8 %fusion = f32[64,3,2,10,130]{0,4,3,2,1:T(8,128)S(1)} fusion(f32[64,3,2,8,1]{0,4,3,2,1:T(1,128)} %collective-permute-done.11, f32[64,3,2,8,1]{0,4,3,2,1:T(1,128)} %collective-permute-done.8, f32[64,3,2,1,128]{0,4,3,2,1:T(8,128)S(1)} %collective-permute-done.10, f32[64,3,2,8,128]{0,4,3,2,1:T(8,128)S(1)} %fusion.9, ...), kind=kLoop, calls=%fused_computation.3 | loop fusion | flops 4492800 | bytes 3987976 | tf_op jit(solution)/shard_map/mul | solution.py:81
  60.4 0.6 fusion.71
  61.1 0.6 pad_maximum_fusion.4
  61.7 2.7 %bitcast_reduce_fusion.1 = (f32[16,3,2,8,8]{4,0,3,2,1:T(8,128)S(1)}, f32[64,3,2,8,128]{0,4,3,2,1:T(8,128)S(1)}) fusion(f32[64,3,2,10,130]{0,4,3,2,1:T(8,128)S(1)} %get-tuple-element.41, f32[64,3,2,10,130]{0,4,3,2,1:T(8,128)S(1)} %get-tuple-element.40, f32[64,3,2,10,130]{0,4,3,2,1:T(8,128)S(1)} %fusion), kind=kLoop, calls=%fused_computation.169 | loop fusion | flops 4319232 | bytes 14180352 | tf_op jit(solution)/shard_map/reduce_sum | solution.py:111
  64.6 0.8 broadcast_multiply_fusion
  65.4 2.5 %gather_fusion = f32[256,64]{1,0:T(8,128)} fusion(f32[64,1024]{0,1:T(8,128)} %bitcast.122, s32[1024]{0:T(1024)} %pad_clamp_fusion), kind=kCustom, calls=%fused_computation | custom fusion | bytes 132096 | tf_op jit(solution)/shard_map/jit(_take)/gather | solution.py:129
  67.9 1.7 %select_bitcast_fusion.1 = f32[64,256]{0,1:T(8,128)} fusion(f32[256,64]{1,0:T(8,128)} %gather_fusion, pred[256]{0:T(512)(128)(4,1)} %compare_and_fusion.1), kind=kLoop, calls=%fused_computation.109 | loop fusion | flops 16384 | bytes 131328 | tf_op jit(solution)/shard_map/jit(_take)/select_n | solution.py:129
  69.6 2.0 %concatenate.33 = f32[68,256]{0,1:T(8,128)} concatenate(f32[64,256]{0,1:T(8,128)} %select_bitcast_fusion.1, f32[1,256]{0,1:T(8,128)} %copy.61, f32[1,256]{0,1:T(8,128)} %copy.62, f32[1,256]{0,1:T(8,128)} %get-tuple-element.47, f32[1,256]{0,1:T(8,128)} %get-tuple-element.46), dimensions={0} | concatenate | bytes 139264 | tf_op jit(solution)/shard_map/concatenate | solution.py:133
  71.6 1.2 collective-permute-start.12
  72.8 4.2 %collective-permute-start.13 = (f32[1,1,68,256]{2,3,1,0:T(8,128)}, f32[1,1,68,256]{2,3,1,0:T(8,128)}, u32[]{:S(2)}, u32[]{:S(2)}) collective-permute-start(f32[1,1,68,256]{2,3,1,0:T(8,128)} %bitcast.124), channel_id=1, source_target_pairs={{8,0},{16,8},{24,16},{32,24},{40,32},{48,40},{56,48},{64,56},{72,6... | collective-permute-start | bytes 208904 | tf_op jit(solution)/shard_map/ppermute | solution.py:45
  77.5 2.1 %copy.64 = f32[1,16,64,3,2,8,8]{2,6,5,4,3,1,0:T(8,128)} copy(f32[1,16,64,3,2,8,8]{2,6,1,5,4,3,0:T(8,128)S(1)} %bitcast.118) | data formatting | bytes 3145728 | tf_op jit(solution)/shard_map/transpose | solution.py:159
  79.6 2.4 %copy.65 = f32[16,64,384]{2,1,0:T(8,128)S(1)} copy(f32[16,64,384]{1,2,0:T(8,128)} %bitcast.119) | data formatting | bytes 3145728 | tf_op jit(solution)/shard_map/reshape | solution.py:159
  82.2 1.0 pad_maximum_fusion.7
  83.2 1.1 collective-permute-start.14
  84.3 1.9 %collective-permute-start.15 = (f32[3,1,68,256]{2,3,1,0:T(8,128)S(1)}, f32[3,1,68,256]{2,3,1,0:T(8,128)}, u32[]{:S(2)}, u32[]{:S(2)}) collective-permute-start(f32[3,1,68,256]{2,3,1,0:T(8,128)S(1)} %pad_maximum_fusion.7), channel_id=1, source_target_pairs={{1,0},{2,1},{3,2},{4,3},{5,4},{6,5},{7,6},{0,7},{9,8},{10,9},{11,1... | collective-permute-start | bytes 626696 | tf_op jit(solution)/shard_map/ppermute | solution.py:45
  86.3 14.0 %collective-permute-done.14 = f32[3,1,68,256]{2,3,1,0:T(8,128)S(1)} collective-permute-done((f32[3,1,68,256]{2,3,1,0:T(8,128)S(1)}, f32[3,1,68,256]{2,3,1,0:T(8,128)S(1)}, u32[]{:S(2)}, u32[]{:S(2)}) %collective-permute-start.14) | collective-permute-done | bytes 208928 | tf_op jit(solution)/shard_map/ppermute | solution.py:44
  100.3 2.3 %collective-permute-done.15 = f32[3,1,68,256]{2,3,1,0:T(8,128)} collective-permute-done((f32[3,1,68,256]{2,3,1,0:T(8,128)S(1)}, f32[3,1,68,256]{2,3,1,0:T(8,128)}, u32[]{:S(2)}, u32[]{:S(2)}) %collective-permute-start.15) | collective-permute-done | bytes 208928 | tf_op jit(solution)/shard_map/ppermute | solution.py:45
  102.6 1.2 pad_maximum_fusion.6
  103.8 7.6 %gather_fusion.1 = f32[2048,68]{1,0:T(8,128)} fusion(f32[68,2304]{0,1:T(8,128)S(1)} %bitcast.117, s32[2048]{0:T(1024)S(1)} %broadcast_clamp_fusion), kind=kCustom, calls=%fused_computation.1 | custom fusion | bytes 1122304 | tf_op jit(solution)/shard_map/jit(_take)/gather | solution.py:146
  111.4 1.6 %select_bitcast_fusion = f32[68,2048]{0,1:T(8,128)S(1)} fusion(f32[2048,68]{1,0:T(8,128)} %gather_fusion.1, pred[2048]{0:T(1024)(128)(4,1)S(1)} %copy-done.6), kind=kLoop, calls=%fused_computation.84 | loop fusion | flops 139264 | bytes 1116160 | tf_op jit(solution)/shard_map/jit(_take)/select_n | solution.py:146
  113.0 2.3 %slice_reduce_fusion = (f32[2048]{0:T(1024)S(1)}, f32[2048]{0:T(1024)S(1)}, f32[2048]{0:T(1024)S(1)}, f32[2048]{0:T(1024)S(1)}) fusion(f32[68,2048]{0,1:T(8,128)S(1)} %select_bitcast_fusion), kind=kLoop, calls=%fused_computation.79 | loop fusion | bytes 65536 | tf_op jit(solution)/shard_map/slice | solution.py:163
  116.0 1.0 fusion.26
  117.5 0.7 fusion.80
  118.8 0.6 fusion.24
  119.5 0.6 fusion.82
  120.1 0.6 fusion.81
  120.8 0.9 convolution_bitcast_fusion.1
  121.7 0.7 fusion.23
  122.3 0.6 fusion.83
  123.0 0.9 convolution_bitcast_fusion
  123.9 0.9 fusion.84
  124.9 3.0 %fusion.20 = f32[16,64,384]{2,1,0:T(8,128)} fusion(f32[16,64,384]{2,1,0:T(8,128)S(1)} %copy.65, f32[16,384]{1,0:T(8,128)S(1)} %copy.56, f32[16,64,64]{2,1,0:T(8,128)S(1)} %fusion.83, f32[16,64]{1,0:T(8,128)S(1)} %broadcast_divide_fusion, f32[16]{0:T(128)S(1)} %get-tuple-element.49), kind=kOutput, calls=%fused_computation.55 | convolution fusion | flops 302907392 | bytes 3436608 | tf_op jit(solution)/shard_map/bif,bik->bkf/dot_general | solution.py:113
  127.9 2.1 %copy.67 = f32[16,64,384]{1,2,0:T(8,128)S(1)} copy(f32[16,64,384]{2,1,0:T(8,128)} %fusion.20) | data formatting | bytes 3145728 | tf_op jit(solution)/shard_map/add | solution.py:113
  130.0 2.1 %copy.78 = f32[64,3,2,1,8,16,8]{0,6,5,4,2,1,3:T(8,128)} copy(f32[64,3,2,1,8,16,8]{0,6,4,2,1,5,3:T(8,128)S(1)} %bitcast.120) | data formatting | bytes 3145728 | tf_op jit(solution)/shard_map/transpose | solution.py:168
  132.1 3.2 %copy.69 = f32[64,3,2,8,128]{4,3,2,1,0:T(8,128)} copy(f32[64,3,2,8,128]{0,4,3,2,1:T(8,128)} %bitcast.121) | data formatting | bytes 3145728 | tf_op jit(solution)/shard_map/reshape | solution.py:168
  (62 shorter events, 7.1 us)
Async XLA Ops:
  0.0 14.7 %copy-start.7 = (s32[1,1,256]{2,1,0:T(1,128)S(1)}, s32[1,1,256]{2,1,0:T(1,128)}, u32[]{:S(2)}) copy-start(s32[1,1,256]{2,1,0:T(1,128)} %param.7) | copy-start | bytes 3076
  0.0 16.8 %copy-start.3 = (s32[1,16,128]{2,1,0:T(8,128)S(1)}, s32[1,16,128]{2,1,0:T(8,128)}, u32[]{:S(2)}) copy-start(s32[1,16,128]{2,1,0:T(8,128)} %param.10) | copy-start | bytes 24580
  3.1 14.9 %collective-permute-start.1 = (f32[64,3,2,1,128]{0,4,3,2,1:T(8,128)}, f32[64,3,2,1,128]{0,4,3,2,1:T(8,128)}, u32[]{:S(2)}, u32[]{:S(2)}) collective-permute-start(f32[64,3,2,1,128]{0,4,3,2,1:T(8,128)} %get-tuple-element.36), channel_id=1, source_target_pairs={{0,8},{8,16},{16,24},{24,32},{32,40},{40,48},{48,56},{56,64},{64,7... | collective-permute-start | bytes 589832 | tf_op jit(solution)/shard_map/ppermute | solution.py:25
  3.1 14.9 %collective-permute-start.2 = (f32[64,3,2,1,128]{0,4,3,2,1:T(8,128)}, f32[64,3,2,1,128]{0,4,3,2,1:T(8,128)}, u32[]{:S(2)}, u32[]{:S(2)}) collective-permute-start(f32[64,3,2,1,128]{0,4,3,2,1:T(8,128)} %get-tuple-element.37), channel_id=1, source_target_pairs={{8,0},{16,8},{24,16},{32,24},{40,32},{48,40},{56,48},{64,56},{72,6... | collective-permute-start | bytes 589832 | tf_op jit(solution)/shard_map/ppermute | solution.py:26
  11.1 7.0 %collective-permute-start = (f32[64,3,2,8,1]{0,4,3,2,1:T(1,128)S(1)}, f32[64,3,2,8,1]{0,4,3,2,1:T(1,128)S(1)}, u32[]{:S(2)}, u32[]{:S(2)}) collective-permute-start(f32[64,3,2,8,1]{0,4,3,2,1:T(1,128)S(1)} %get-tuple-element.38), channel_id=1, source_target_pairs={{0,1},{1,2},{2,3},{3,4},{4,5},{5,6},{6,7},{7,0},{8,9},{9,10},{10,1... | collective-permute-start | bytes 36872 | tf_op jit(solution)/shard_map/ppermute | solution.py:25
  11.8 6.2 %collective-permute-start.3 = (f32[64,3,2,8,1]{0,4,3,2,1:T(1,128)S(1)}, f32[64,3,2,8,1]{0,4,3,2,1:T(1,128)S(1)}, u32[]{:S(2)}, u32[]{:S(2)}) collective-permute-start(f32[64,3,2,8,1]{0,4,3,2,1:T(1,128)S(1)} %get-tuple-element.39), channel_id=1, source_target_pairs={{1,0},{2,1},{3,2},{4,3},{5,4},{6,5},{7,6},{0,7},{9,8},{10,9},{11,1... | collective-permute-start | bytes 36872 | tf_op jit(solution)/shard_map/ppermute | solution.py:26
  18.0 18.5 %copy-start.5 = (f32[130]{0:T(256)}, f32[130]{0:T(256)S(1)}, u32[]{:S(2)}) copy-start(f32[130]{0:T(256)S(1)} %and_convert_fusion) | copy-start | bytes 1564
  24.3 12.2 %collective-permute-start.5 = (f32[64,3,2,1,128]{0,4,3,2,1:T(8,128)S(1)}, f32[64,3,2,1,128]{0,4,3,2,1:T(8,128)S(1)}, u32[]{:S(2)}, u32[]{:S(2)}) collective-permute-start(f32[64,3,2,1,128]{0,4,3,2,1:T(8,128)S(1)} %get-tuple-element.32), channel_id=1, source_target_pairs={{0,8},{8,16},{16,24},{24,32},{32,40},{40,48},{48,56},{56,64},{64,7... | collective-permute-start | bytes 589832 | tf_op jit(solution)/shard_map/ppermute | solution.py:25
  26.5 10.0 %collective-permute-start.6 = (f32[64,3,2,1,128]{0,4,3,2,1:T(8,128)S(1)}, f32[64,3,2,1,128]{0,4,3,2,1:T(8,128)S(1)}, u32[]{:S(2)}, u32[]{:S(2)}) collective-permute-start(f32[64,3,2,1,128]{0,4,3,2,1:T(8,128)S(1)} %get-tuple-element.33), channel_id=1, source_target_pairs={{8,0},{16,8},{24,16},{32,24},{40,32},{48,40},{56,48},{64,56},{72,6... | collective-permute-start | bytes 589832 | tf_op jit(solution)/shard_map/ppermute | solution.py:26
  29.8 5.1 %collective-permute-start.4 = (f32[64,3,2,8,1]{0,4,3,2,1:T(1,128)S(1)}, f32[64,3,2,8,1]{0,4,3,2,1:T(1,128)S(1)}, u32[]{:S(2)}, u32[]{:S(2)}) collective-permute-start(f32[64,3,2,8,1]{0,4,3,2,1:T(1,128)S(1)} %get-tuple-element.34), channel_id=1, source_target_pairs={{0,1},{1,2},{2,3},{3,4},{4,5},{5,6},{6,7},{7,0},{8,9},{9,10},{10,1... | collective-permute-start | bytes 36872 | tf_op jit(solution)/shard_map/ppermute | solution.py:25
  30.8 5.7 %collective-permute-start.7 = (f32[64,3,2,8,1]{0,4,3,2,1:T(1,128)S(1)}, f32[64,3,2,8,1]{0,4,3,2,1:T(1,128)S(1)}, u32[]{:S(2)}, u32[]{:S(2)}) collective-permute-start(f32[64,3,2,8,1]{0,4,3,2,1:T(1,128)S(1)} %get-tuple-element.35), channel_id=1, source_target_pairs={{1,0},{2,1},{3,2},{4,3},{5,4},{6,5},{7,6},{0,7},{9,8},{10,9},{11,1... | collective-permute-start | bytes 36872 | tf_op jit(solution)/shard_map/ppermute | solution.py:26
  38.6 11.4 %copy-start.8 = (s32[256,1]{0,1:T(1,128)S(1)}, s32[256,1]{0,1:T(1,128)}, u32[]{:S(2)}) copy-start(s32[256,1]{0,1:T(1,128)} %compare_select_fusion.2) | copy-start | bytes 3076
  42.7 11.3 %collective-permute-start.10 = (f32[64,3,2,1,128]{0,4,3,2,1:T(8,128)}, f32[64,3,2,1,128]{0,4,3,2,1:T(8,128)S(1)}, u32[]{:S(2)}, u32[]{:S(2)}) collective-permute-start(f32[64,3,2,1,128]{0,4,3,2,1:T(8,128)} %get-tuple-element.29), channel_id=1, source_target_pairs={{8,0},{16,8},{24,16},{32,24},{40,32},{48,40},{56,48},{64,56},{72,6... | collective-permute-start | bytes 589832 | tf_op jit(solution)/shard_map/ppermute | solution.py:26
  47.4 11.3 %collective-permute-start.9 = (f32[64,3,2,1,128]{0,4,3,2,1:T(8,128)}, f32[64,3,2,1,128]{0,4,3,2,1:T(8,128)}, u32[]{:S(2)}, u32[]{:S(2)}) collective-permute-start(f32[64,3,2,1,128]{0,4,3,2,1:T(8,128)} %get-tuple-element.28), channel_id=1, source_target_pairs={{0,8},{8,16},{16,24},{24,32},{32,40},{40,48},{48,56},{56,64},{64,7... | collective-permute-start | bytes 589832 | tf_op jit(solution)/shard_map/ppermute | solution.py:25
  48.0 5.6 %collective-permute-start.11 = (f32[64,3,2,8,1]{0,4,3,2,1:T(1,128)}, f32[64,3,2,8,1]{0,4,3,2,1:T(1,128)}, u32[]{:S(2)}, u32[]{:S(2)}) collective-permute-start(f32[64,3,2,8,1]{0,4,3,2,1:T(1,128)} %get-tuple-element.31), channel_id=1, source_target_pairs={{1,0},{2,1},{3,2},{4,3},{5,4},{6,5},{7,6},{0,7},{9,8},{10,9},{11,1... | collective-permute-start | bytes 36872 | tf_op jit(solution)/shard_map/ppermute | solution.py:26
  48.9 5.1 %collective-permute-start.8 = (f32[64,3,2,8,1]{0,4,3,2,1:T(1,128)}, f32[64,3,2,8,1]{0,4,3,2,1:T(1,128)}, u32[]{:S(2)}, u32[]{:S(2)}) collective-permute-start(f32[64,3,2,8,1]{0,4,3,2,1:T(1,128)} %get-tuple-element.30), channel_id=1, source_target_pairs={{0,1},{1,2},{2,3},{3,4},{4,5},{5,6},{6,7},{7,0},{8,9},{9,10},{10,1... | collective-permute-start | bytes 36872 | tf_op jit(solution)/shard_map/ppermute | solution.py:25
  71.6 10.5 %collective-permute-start.12 = (f32[1,1,68,256]{2,3,1,0:T(8,128)}, f32[1,1,68,256]{2,3,1,0:T(8,128)}, u32[]{:S(2)}, u32[]{:S(2)}) collective-permute-start(f32[1,1,68,256]{2,3,1,0:T(8,128)} %bitcast.123), channel_id=1, source_target_pairs={{0,8},{8,16},{16,24},{24,32},{32,40},{40,48},{48,56},{56,64},{64,7... | collective-permute-start | bytes 208904 | tf_op jit(solution)/shard_map/ppermute | solution.py:44
  72.8 9.4 %collective-permute-start.13 = (f32[1,1,68,256]{2,3,1,0:T(8,128)}, f32[1,1,68,256]{2,3,1,0:T(8,128)}, u32[]{:S(2)}, u32[]{:S(2)}) collective-permute-start(f32[1,1,68,256]{2,3,1,0:T(8,128)} %bitcast.124), channel_id=1, source_target_pairs={{8,0},{16,8},{24,16},{32,24},{40,32},{48,40},{56,48},{64,56},{72,6... | collective-permute-start | bytes 208904 | tf_op jit(solution)/shard_map/ppermute | solution.py:45
  79.6 2.6 %copy-start = (f32[68,256]{0,1:T(8,128)S(1)}, f32[68,256]{0,1:T(8,128)}, u32[]{:S(2)}) copy-start(f32[68,256]{0,1:T(8,128)} %concatenate.33) | copy-start | bytes 208900
  83.2 17.1 %collective-permute-start.14 = (f32[3,1,68,256]{2,3,1,0:T(8,128)S(1)}, f32[3,1,68,256]{2,3,1,0:T(8,128)S(1)}, u32[]{:S(2)}, u32[]{:S(2)}) collective-permute-start(f32[3,1,68,256]{2,3,1,0:T(8,128)S(1)} %pad_maximum_fusion.7), channel_id=1, source_target_pairs={{0,1},{1,2},{2,3},{3,4},{4,5},{5,6},{6,7},{7,0},{8,9},{9,10},{10,1... | collective-permute-start | bytes 626696 | tf_op jit(solution)/shard_map/ppermute | solution.py:44
  84.3 18.3 %collective-permute-start.15 = (f32[3,1,68,256]{2,3,1,0:T(8,128)S(1)}, f32[3,1,68,256]{2,3,1,0:T(8,128)}, u32[]{:S(2)}, u32[]{:S(2)}) collective-permute-start(f32[3,1,68,256]{2,3,1,0:T(8,128)S(1)} %pad_maximum_fusion.7), channel_id=1, source_target_pairs={{1,0},{2,1},{3,2},{4,3},{5,4},{6,5},{7,6},{0,7},{9,8},{10,9},{11,1... | collective-permute-start | bytes 626696 | tf_op jit(solution)/shard_map/ppermute | solution.py:45
  103.7 7.6 %copy-start.6 = (pred[2048]{0:T(1024)(128)(4,1)S(1)}, pred[2048]{0:T(1024)(128)(4,1)}, u32[]{:S(2)}) copy-start(pred[2048]{0:T(1024)(128)(4,1)} %compare_and_fusion) | copy-start | bytes 6148
  113.0 2.7 %copy-start.9 = (s32[1,16]{1,0:T(1,128)S(1)}, s32[1,16]{1,0:T(1,128)}, u32[]{:S(2)}) copy-start(s32[1,16]{1,0:T(1,128)} %param.11) | copy-start | bytes 196
  113.0 2.7 %copy-start.10 = (f32[16]{0:T(128)S(1)}, f32[16]{0:T(128)}, u32[]{:S(2)}) copy-start(f32[16]{0:T(128)} %convert_add_fusion) | copy-start | bytes 196
  113.0 3.0 %copy-start.4 = (f32[64,64]{1,0:T(8,128)S(1)}, f32[64,64]{1,0:T(8,128)}, u32[]{:S(2)}) copy-start(f32[64,64]{1,0:T(8,128)} %fusion.43) | copy-start | bytes 49156
  115.3 1.7 %copy-start.1 = (f32[64,64]{1,0:T(8,128)S(1)}, f32[64,64]{1,0:T(8,128)}, u32[]{:S(2)}) copy-start(f32[64,64]{1,0:T(8,128)} %fusion.45) | copy-start | bytes 49156
  115.3 1.7 %copy-start.2 = (f32[64,64]{1,0:T(8,128)S(1)}, f32[64,64]{1,0:T(8,128)}, u32[]{:S(2)}) copy-start(f32[64,64]{1,0:T(8,128)} %fusion.44) | copy-start | bytes 49156
where the time goes:
time: 136 us; the launch traced here: 135 us
  local copies, waits for them, and re-layouts  34.7 us (26%)
  starting transfers between devices  34.4 us (25%)
  other arithmetic  29.4 us (22%)
  waiting for transfers between devices  24.5 us (18%)
  matrix products  11.8 us (9%)
    ppermute x6, starting transfers between devices, padded_2(): lax.ppermute(initial, axis, [(b, a) for a, b in up])  21 us
    ppermute x2, waiting for transfers between devices, padded_3(): before = lax.ppermute(last, axis, up)  14 us
    gather x1, local copies, waits for them, and re-layouts, local(): jnp.take(obs_table, entries.reshape(-1), axis=1)  7.64 us
    ppermute x6, waiting for transfers between devices, padded_2(): lax.ppermute(last, axis, up)  6.59 us
    sub x2, other arithmetic, friedrichs_step(): 0.25 * neighbours  6.23 us
    ppermute x2, starting transfers between devices, padded_3(): after = lax.ppermute(initial, axis, down)  6.03 us
    ppermute x6, starting transfers between devices, padded_2(): lax.ppermute(last, axis, up)  5.08 us
    mul x3, other arithmetic, cut_outside(): return padded * inside.astype(padded.dtype)  4.41 us
  transfers between devices with their start and end apart: 16, of which 6 were waited for; matrix products, arithmetic and copies ran while one was open for 10% of the time, Pallas kernels for 0%

commit v1 on v0

v1 whole, which is shorter than its diff:
```python
import jax
import jax.numpy as jnp
from jax import lax
from jax.experimental import pallas as pl
from jax.experimental.pallas import tpu as pltpu
from jax.sharding import PartitionSpec as P

K = 64
CX = 8
CY = 128
W = 3
SLOTS = 256
CAP = 128
PATCHES = 16
PAIRS = 8
LATP = 160
LAT0 = 16
F32 = jnp.float32
BF = jnp.bfloat16
VM = pl.BlockSpec(memory_space=pltpu.VMEM)
SM = pl.BlockSpec(memory_space=pltpu.SMEM)
LIMIT = 60 * 1024 * 1024


def call(kernel, outs, ins, scratch=(), cost=None):
    return pl.pallas_call(
        kernel,
        out_shape=[jax.ShapeDtypeStruct(s, F32) for s in outs],
        in_specs=ins,
        out_specs=[VM] * len(outs),
        scratch_shapes=list(scratch),
        compiler_params=pltpu.CompilerParams(vmem_limit_bytes=LIMIT),
        cost_estimate=cost,
    )


def split(x):
    hi = x.astype(BF)
    return hi, (x - hi.astype(F32)).astype(BF)


def dot(a, b):
    return lax.dot_general(a, b, (((1,), (0,)), ((), ())), preferred_element_type=F32)


def dot_t(a, b):
    return lax.dot_general(a, b, (((1,), (1,)), ((), ())), preferred_element_type=F32)


def mm3(a, b, d=dot):
    return d(a[0], b[0]) + d(a[0], b[1]) + d(a[1], b[0])


def relayout(s_ref, x_ref, st_ref, t_ref, eoff_ref, eon_ref, ga_ref, gb_ref):
    px = s_ref[0]
    py = s_ref[1]
    for f in range(3):
        for lon in range(CX):
            low = x_ref[pl.ds(f * 16 + lon, K, stride=48), :]
            high = x_ref[pl.ds(f * 16 + 8 + lon, K, stride=48), :]
            t_ref[pl.ds((f * CX + lon) * CY, CY), :] = jnp.concatenate([low, high], axis=0).T
    start_off = jnp.where(px == 0, 0, CX - W)
    start_on = (CX - W) - start_off
    for f in range(3):
        for ref, start in ((eoff_ref, start_off), (eon_ref, start_on)):
            row = pl.multiple_of((f * CX + start) * CY, CY)
            ref[pl.ds(f * W * CY, W * CY), :] = t_ref[pl.ds(row, W * CY), :]
    for f in range(3):
        for la in range(W):
            south = t_ref[pl.ds(f * CX * CY + la, CX, stride=CY), :]
            north = t_ref[pl.ds(f * CX * CY + CY - W + la, CX, stride=CY), :]
            row = (f * W + la) * CX
            ga_ref[pl.ds(row, CX), :] = jnp.where(py == 0, north, south)
            gb_ref[pl.ds(row, CX), :] = jnp.where(py == 0, south, north)
    ga_ref[pl.ds(72, 8), :] = st_ref[...]
    gb_ref[pl.ds(72, 8), :] = st_ref[...]


def corners(s_ref, st_ref, ga_ref, gb_ref, coff_ref, con_ref):
    px = s_ref[0]
    for k, ref in enumerate((ga_ref, gb_ref)):
        for c in range(9):
            v = ref[pl.ds(c * CX, CX), :]
            lo = v[0:W]
            hi = v[CX - W : CX]
            row = (k * 9 + c) * W
            coff_ref[pl.ds(row, W), :] = jnp.where(px == 0, lo, hi)
            con_ref[pl.ds(row, W), :] = jnp.where(px == 0, hi, lo)
    pad = jnp.zeros((2, 128), F32)
    coff_ref[pl.ds(54, 2), :] = pad
    con_ref[pl.ds(54, 2), :] = pad
    for i, v in enumerate((st_ref[...], ga_ref[pl.ds(72, 8), :], gb_ref[pl.ds(72, 8), :])):
        coff_ref[pl.ds(56 + 8 * i, 8), :] = v
        con_ref[pl.ds(56 + 8 * i, 8), :] = v


def forecast(
    s_ref, col_ref, t_ref, roff_ref, ron_ref, ga_ref, gb_ref, coff_ref, con_ref,
    out_ref, obs_ref, q_ref, p_ref, bp_ref, bm_ref, tmp_ref,
):
    px = s_ref[0]
    py = s_ref[1]
    first = s_ref[2]
    last = s_ref[3]
    off_at = jnp.where(px == 0, 0, CX + W)
    on_at = (CX + W) - off_at
    NL = CX + 2 * W

    def base(f, lon):
        return (f * NL + lon) * LATP

    for f in range(3):
        for lon in range(CX):
            q_ref[pl.ds(base(f, lon + W) + LAT0, CY), :] = t_ref[pl.ds((f * CX + lon) * CY, CY), :]
        for ref, at in ((roff_ref, off_at), (ron_ref, on_at)):
            for i in range(W):
                row = pl.multiple_of(base(f, at + i) + LAT0, 8)
                q_ref[pl.ds(row, CY), :] = ref[pl.ds((f * W + i) * CY, CY), :]
    z5 = jnp.zeros((5, 128), F32)

    def put(f, lon, a, b):
        north = jnp.where(py == 0, a, b)
        south = jnp.where(py == 0, b, a)
        row = base(f, lon) + LAT0
        if not isinstance(row, int):
            row = pl.multiple_of(row, 8)
        q_ref[pl.ds(row - 8, 8), :] = jnp.concatenate([z5, south], axis=0)
        q_ref[pl.ds(row + CY, 8), :] = jnp.concatenate([north, z5], axis=0)

    for f in range(3):
        for lon in range(CX):
            a = ga_ref[pl.ds(f * W * CX + lon, W, stride=CX), :]
            b = gb_ref[pl.ds(f * W * CX + lon, W, stride=CX), :]
            put(f, lon + W, a, b)
        for ref, at in ((coff_ref, off_at), (con_ref, on_at)):
            for i in range(W):
                a = ref[pl.ds(f * 9 + i, W, stride=W), :]
                b = ref[pl.ds(27 + f * 9 + i, W, stride=W), :]
                put(f, at + i, a, b)

    for step in range(3):
        lo, hi = step, NL - 1 - step

        def flux(tile, carry):
            row = pl.multiple_of(tile * 8, 8)
            prev = []
            for lon in range(lo, hi + 1):
                hd = q_ref[pl.ds(base(0, lon) + row, 8), :]
                m = q_ref[pl.ds(base(1, lon) + row, 8), :]
                n = q_ref[pl.ds(base(2, lon) + row, 8), :]
                h = 1.0 + hd
                rh = 1.0 / h
                m5 = 0.15 * m
                n5 = 0.15 * n
                u5 = m5 * rh
                v5 = n5 * rh
                cross = u5 * n
                p5 = (0.075 * h) * h
                fm = u5 * m + p5
                gn = v5 * n + p5
                th, tm, tn = 0.25 * hd, 0.25 * m, 0.25 * n
                plus = (th + m5, tm + fm, tn + cross)
                minus = (th - m5, tm - fm, tn - cross)
                if lo < lon < hi:
                    for f, (t, g) in enumerate(((th, n5), (tm, cross), (tn, gn))):
                        bp_ref[pl.ds(base(f, lon) + row, 8), :] = t + g
                        bm_ref[pl.ds(base(f, lon) + row, 8), :] = t - g
                if len(prev) == 2:
                    for f in range(3):
                        p_ref[pl.ds(base(f, lon - 1) + row, 8), :] = prev[0][f] + minus[f]
                prev = (prev + [plus])[-2:]
            return carry

        lax.fori_loop(1, LATP // 8 - 1, flux, 0)
        final = step == 2

        def combine(tile, carry):
            row = pl.multiple_of(tile * 8, 8)
            outside = ((tile == 1) & (first == 1)) | ((tile == 18) & (last == 1))
            for lon in range(lo + 1, hi):
                for f in range(3):
                    at = base(f, lon) + row
                    v = (
                        p_ref[pl.ds(at, 8), :]
                        + bm_ref[pl.ds(at + 1, 8), :]
                        + bp_ref[pl.ds(at - 1, 8), :]
                    )
                    if final:
                        out_ref[pl.ds((f * CX + lon - W) * CY + row - LAT0, 8), :] = v
                    else:
                        q_ref[pl.ds(at, 8), :] = jnp.where(outside, 0.0, v)
            return carry

        if final:
            lax.fori_loop(2, 18, combine, 0)
        else:
            lax.fori_loop(1, 19, combine, 0)

    sub = lax.broadcasted_iota(jnp.int32, (8, 128), 0)
    lane = lax.broadcasted_iota(jnp.int32, (8, 128), 1)

    def rows8(start):
        v = jnp.broadcast_to(out_ref[pl.ds(col_ref[start], 1), :], (8, 128))
        for s in range(1, 8):
            w = jnp.broadcast_to(out_ref[pl.ds(col_ref[start + s], 1), :], (8, 128))
            v = jnp.where(sub == s, w, v)
        return 0.5 * (v + pltpu.roll(v, 64, 1))

    def pick(g, carry):
        left = rows8(g * 8)
        right = rows8(128 + g * 8)
        obs_ref[pl.ds(pl.multiple_of(g * 8, 8), 8), :] = jnp.where(lane < 64, left, right)
        return carry

    lax.fori_loop(0, 16, pick, 0)


def gather_pair(list_ref, tab_ref, y_ref, pair, groups):
    sub = lax.broadcasted_iota(jnp.int32, (8, 128), 0)
    left = lax.broadcasted_iota(jnp.int32, (8, 128), 1) < 64
    masks = [(sub == s) & left for s in range(8)] + [(sub == s) & (~left) for s in range(8)]

    def body(g, carry):
        at = pair * (2 * CAP) + g * 8
        v = None
        for half in range(2):
            for s in range(8):
                idx = list_ref[at + half * CAP + s]
                w = jnp.broadcast_to(tab_ref[pl.ds(idx, 1), :], (8, 128))
                v = w if v is None else jnp.where(masks[half * 8 + s], w, v)
        y_ref[pl.ds(pl.multiple_of(g * 8, 8), 8), :] = v
        return carry

    lax.fori_loop(0, groups, body, 0)


def tile_codes(px, py):
    dx_on = jnp.where(px == 0, 1, -1)
    dy_a = jnp.where(py == 0, 1, -1)
    return dx_on, dy_a


def weights(s_ref, cnt_ref, list_ref, st_ref, ga_ref, gb_ref, coff_ref, con_ref,
            r_ref, v_ref, tab_ref, y_ref):
    px = s_ref[0]
    py = s_ref[1]
    dx_on, dy_a = tile_codes(px, py)
    sources = [(st_ref[...], 0, 0), (ga_ref[pl.ds(72, 8), :], 0, dy_a), (gb_ref[pl.ds(72, 8), :], 0, -dy_a)]
    for ref, dx in ((coff_ref, -dx_on), (con_ref, dx_on)):
        for i, dy in enumerate((0, dy_a, -dy_a)):
            sources.append((ref[pl.ds(56 + 8 * i, 8), :], dx, dy))
    zero = jnp.zeros((61, 128), F32)
    for rows, dx, dy in sources:
        code = (dx + 1) * 3 + dy + 1
        fx = jnp.asarray(dx * CX, jnp.int32).astype(F32)
        fy = jnp.asarray(dy * CY, jnp.int32).astype(F32)
        value, prec, col = rows[0:2], rows[2:4], rows[4:6]
        lon = jnp.floor(col * (1.0 / CY))
        lat = col - lon * CY
        ox = (fx + lon - 3.5) * (1.0 / CX)
        wx = prec * jnp.exp(-(ox * ox))
        y = fy + lat
        for half in range(2):
            h = slice(half, half + 1)
            block = jnp.concatenate([wx[h], y[h], value[h], zero], axis=0)
            block = jnp.concatenate([block, block], axis=0)
            at = code * SLOTS + half * 128
            if not isinstance(at, int):
                at = pl.multiple_of(at, 128)
            tab_ref[pl.ds(at, 128), :] = block.T

    left = lax.broadcasted_iota(jnp.int32, (CAP, 128), 1) < 64
    entry = lax.broadcasted_iota(jnp.int32, (CAP, 128), 0)

    def body(pair, carry):
        gather_pair(list_ref, tab_ref, y_ref, pair, 16)
        g = y_ref[...]

        def both(i):
            a = jnp.broadcast_to(g[:, i : i + 1], (CAP, 128))
            b = jnp.broadcast_to(g[:, 64 + i : 65 + i], (CAP, 128))
            return jnp.where(left, a, b)

        centre = (pair * 16).astype(F32) + 3.5
        oy = (both(1) - jnp.where(left, centre, centre + 8.0)) * (1.0 / CY)
        count = jnp.where(left, cnt_ref[2 * pair], cnt_ref[2 * pair + 1])
        r = jnp.where(entry < count, both(0) * jnp.exp(-(oy * oy)), 0.0)
        at = pl.ds(pl.multiple_of(pair * CAP, CAP), CAP)
        r_ref[at, :] = r
        v_ref[at, :] = both(2)
        return carry

    lax.fori_loop(0, PAIRS, body, 0)


def analysis(
    s_ref, cnt_ref, list_ref, r_ref, v_ref, own_ref, oa_ref, ob_ref, on_ref, off_ref, fa_ref, fb_ref,
    t_ref, out_ref, tab_ref, y_ref, a_ref, z_ref, ya_ref, f_ref, c_ref, m_ref, o_ref,
):
    px = s_ref[0]
    py = s_ref[1]
    dx_on, dy_a = tile_codes(px, py)
    lane8 = lax.broadcasted_iota(jnp.int32, (128, 128), 1) < 64

    def unpack(packed, dx, dy):
        rolled = pltpu.roll(packed, 64, 1)
        at = pl.multiple_of(((dx + 1) * 3 + dy + 1) * SLOTS, SLOTS)
        tab_ref[pl.ds(at, 128), :] = jnp.where(lane8, packed, rolled)
        tab_ref[pl.ds(at + 128, 128), :] = jnp.where(lane8, rolled, packed)

    zero = jnp.int32(0)
    unpack(own_ref[...], zero, zero)
    unpack(oa_ref[...], zero, dy_a)
    unpack(ob_ref[...], zero, -dy_a)
    for i, dy in enumerate((zero, dy_a, -dy_a)):
        unpack(on_ref[pl.ds(i * 128, 128), :], dx_on, dy)
    unpack(off_ref[...], -dx_on, zero)
    unpack(fa_ref[...], -dx_on, dy_a)
    unpack(fb_ref[...], -dx_on, -dy_a)

    row = lax.broadcasted_iota(jnp.int32, (128, 128), 0)
    lane = lax.broadcasted_iota(jnp.int32, (128, 128), 1)
    same = (row < 64) == (lane < 64)
    eye = jnp.where(row == lane, 1.0, 0.0).astype(F32)
    mean_of = jnp.where(same, 1.0 / 64, 0.0).astype(BF)
    lane1 = lax.broadcasted_iota(jnp.int32, (1, 128), 1)
    y_ref[...] = jnp.zeros_like(y_ref)

    def gram(pair, carry):
        most = jnp.maximum(cnt_ref[2 * pair], cnt_ref[2 * pair + 1])
        gather_pair(list_ref, tab_ref, y_ref, pair, (most + 7) // 8)
        at = pl.ds(pl.multiple_of(pair * CAP, CAP), CAP)
        y = y_ref[...]
        yh, yl = split(y)
        mean = dot(yh, mean_of) + dot(yl, mean_of)
        pert = y - mean
        r = r_ref[at, :]
        rp = r * pert
        force = jnp.sum(rp * (v_ref[at, :] - mean), axis=0, keepdims=True)
        rt = split(rp.T)
        g = mm3(rt, split(pert))
        diag = jnp.sum(g * eye, axis=0, keepdims=True)
        ca = 63.0 + jnp.sum(jnp.where(lane1 < 64, diag, 0.0), axis=1, keepdims=True)
        cb = 63.0 + jnp.sum(jnp.where(lane1 < 64, 0.0, diag), axis=1, keepdims=True)
        c = jnp.where(lane1 < 64, ca, cb)
        a_ref[at, :] = jnp.where(same, (g + 63.0 * eye) / c, 0.0)
        f_ref[pl.ds(pair, 1), :] = force
        c_ref[pl.ds(pair, 1), :] = c
        return carry

    lax.fori_loop(0, PAIRS, gram, 0)

    def at(p):
        return pl.ds(p * CAP, CAP)

    pairs = range(PAIRS)
    for p in pairs:
        a = a_ref[at(p), :]
        s = 1.5 * eye - 0.5 * a
        z_ref[at(p), :] = s
        ya_ref[at(p), :] = mm3(split(a), split(s))
    for p in pairs:
        z = split(z_ref[at(p), :])
        y = split(ya_ref[at(p), :])
        a_ref[at(p), :] = 1.5 * eye - 0.5 * mm3(z, y)
    for p in pairs:
        s = split(a_ref[at(p), :])
        z = split(z_ref[at(p), :])
        y = split(ya_ref[at(p), :])
        z_ref[at(p), :] = mm3(s, z)
        ya_ref[at(p), :] = mm3(s, y)
    for p in pairs:
        z = split(z_ref[at(p), :])
        y = split(ya_ref[at(p), :])
        a_ref[at(p), :] = 1.5 * eye - 0.5 * mm3(z, y)
    for p in pairs:
        s = split(a_ref[at(p), :])
        z = split(z_ref[at(p), :])
        z = mm3(s, z)
        c = c_ref[pl.ds(p, 1), :]
        g = jnp.sum(z * f_ref[pl.ds(p, 1), :], axis=1, keepdims=True)
        wbar = jnp.sum(z * g, axis=0, keepdims=True) / c
        wt = z * jnp.sqrt(63.0 / c) + wbar
        wt = jnp.where(same, wt, 0.0)
        mean = jnp.sum(wt, axis=1, keepdims=True) * (1.0 / 64)
        m = jnp.where(same, wt + (1.0 / 64) - mean, 0.0)
        ma, mb = m[0:64], m[64:128]
        m_ref[pl.ds(2 * p * 128, 64), :] = ma
        m_ref[pl.ds(2 * p * 128 + 64, 64), :] = pltpu.roll(ma, 64, 1)
        m_ref[pl.ds((2 * p + 1) * 128, 64), :] = pltpu.roll(mb, 64, 1)
        m_ref[pl.ds((2 * p + 1) * 128 + 64, 64), :] = mb

    def update(p, carry):
        m = split(m_ref[pl.ds(pl.multiple_of(p * 128, 128), 128), :])
        rows = [t_ref[pl.ds(pl.multiple_of(i * CY + p * 8, 8), 8), :] for i in range(24)]
        x = split(jnp.concatenate(rows, axis=0))
        o = mm3(x, m, dot_t)
        for i in range(24):
            o_ref[pl.ds(pl.multiple_of(i * CY + p * 8, 8), 8), :] = o[i * 8 : i * 8 + 8]
        return carry

    lax.fori_loop(0, PATCHES, update, 0)
    for f in range(3):
        for lon in range(CX):
            v = o_ref[pl.ds((f * CX + lon) * CY, CY), :].T
            out_ref[pl.ds(f * 16 + lon, K, stride=48), :] = v[0:64]
            out_ref[pl.ds(f * 16 + 8 + lon, K, stride=48), :] = v[64:128]


def swaps(size, odd, ring):
    pairs = []
    for i in range(odd, size, 2):
        j = i + 1
        if j >= size:
            if not ring:
                continue
            j %= size
        pairs += [(i, j), (j, i)]
    return pairs


def local(prior_members, obs_column, obs_value, obs_precision, obs_list, patch_count):
    gx, gy = lax.axis_index("gx"), lax.axis_index("gy")
    nx, ny = lax.axis_size("gx"), lax.axis_size("gy")
    scalars = jnp.stack(
        [gx % 2, gy % 2, (gy == 0).astype(jnp.int32), (gy == ny - 1).astype(jnp.int32)]
    ).astype(jnp.int32)

    def on(x):
        return lax.ppermute(x, "gx", swaps(nx, 0, True))

    def off(x):
        return lax.ppermute(x, "gx", swaps(nx, 1, True))

    def gya(x):
        return lax.ppermute(x, "gy", swaps(ny, 0, False))

    def gyb(x):
        return lax.ppermute(x, "gy", swaps(ny, 1, False))

    columns = obs_column[0, 0]
    static = jnp.concatenate(
        [
            obs_value.reshape(2, 128),
            obs_precision.reshape(2, 128),
            columns.astype(F32).reshape(2, 128),
            jnp.zeros((2, 128), F32),
        ],
        axis=0,
    )
    entries = obs_list.reshape(PATCHES * CAP)
    counts = patch_count.reshape(PATCHES)
    x = prior_members.reshape(3072, 128)
    t, eoff, eon, ga, gb = call(
        relayout,
        [(3072, 128), (1152, 128), (1152, 128), (80, 128), (80, 128)],
        [SM, VM, VM],
    )(scalars, x, static)
    roff = off(eoff)
    ra = gya(ga)
    rb = gyb(gb)
    ron = on(eon)
    coff, con = call(corners, [(80, 128), (80, 128)], [SM, VM, VM, VM])(scalars, static, ra, rb)
    rcoff = off(coff)
    rcon = on(con)
    cells = 3 * 14 * LATP
    state, obs = call(
        forecast,
        [(3072, 128), (128, 128)],
        [SM, SM] + [VM] * 7,
        [pltpu.VMEM((cells, 128), F32)] * 4 + [pltpu.VMEM((8, 128), F32)],
    )(scalars, columns, t, roff, ron, ra, rb, rcoff, rcon)
    r, v = call(
        weights,
        [(1024, 128), (1024, 128)],
        [SM, SM, SM] + [VM] * 5,
        [pltpu.VMEM((9 * SLOTS, 128), F32), pltpu.VMEM((CAP, 128), F32)],
    )(scalars, counts, entries, static, ra, rb, rcoff, rcon)
    o_off = off(obs)
    o_a = gya(obs)
    o_b = gyb(obs)
    o_on = on(jnp.concatenate([obs, o_a, o_b], axis=0))
    f_a = gya(o_off)
    f_b = gyb(o_off)
    sq = pltpu.VMEM((1024, 128), F32)
    small = pltpu.VMEM((8, 128), F32)
    (out,) = call(
        analysis,
        [(3072, 128)],
        [SM, SM, SM] + [VM] * 10,
        [
            pltpu.VMEM((9 * SLOTS, 128), F32),
            pltpu.VMEM((CAP, 128), F32),
            sq,
            sq,
            sq,
            small,
            small,
            pltpu.VMEM((2048, 128), F32),
            pltpu.VMEM((3072, 128), F32),
        ],
    )(scalars, counts, entries, r, v, obs, o_a, o_b, o_on, o_off, f_a, f_b, state)
    return out.reshape(prior_members.shape)


def solution(mesh):
    return jax.shard_map(
        local,
        mesh=mesh,
        in_specs=(
            P(None, None, None, "gx", "gy"),
            P("gx", "gy", None),
            P("gx", "gy", None),
            P("gx", "gy", None),
            P("gx", "gy", None),
            P("gx", "gy"),
        ),
        out_specs=P(None, None, None, "gx", "gy"),
        check_vma=False,
    )
```

time: 136 us -> 90.8 us (0.67)
  Pallas kernels: 0 us -> 36 us
  local copies, waits for them, and re-layouts: 34.7 us -> 2.41 us
  other arithmetic: 29.4 us -> 3.57 us
  waiting for transfers between devices: 24.5 us -> 11.2 us
  matrix products: 11.8 us -> 0 us
  starting transfers between devices: 34.4 us -> 36.1 us
    pallas_call x0 -> x5, Pallas kernels: none -> 36 us  [the longest x1 13.6 us: local(): call(analysis, [(3072, 128)], [SM, SM, SM] + [VM] * 10, [pltpu.VMEM((9 *...]
    ppermute x16 -> x12, waiting for transfers between devices: 24.5 us -> 11.2 us  [the longest x3 4.7 us: gyb(): return lax.ppermute(x, 'gy', swaps(ny, 1, False))]
    dot_general x13 -> x0, matrix products: 11.8 us -> none  [the longest x1 2.99 us: analyse(): jnp.einsum('bif,bik->bkf', field_pert, combined, precision=highest)]
    gather x2 -> x0, local copies, waits for them, and re-layouts: 10.2 us -> none  [the longest x1 7.64 us: local(): jnp.take(obs_table, entries.reshape(-1), axis=1)]
    sub x2 -> x0, other arithmetic: 6.23 us -> none  [friedrichs_step(): 0.25 * neighbours]
    mul x6 -> x0, other arithmetic: 5.72 us -> none  [the longest x3 4.41 us: cut_outside(): return padded * inside.astype(padded.dtype)]
    reshape x2 -> x0, local copies, waits for them, and re-layouts: 5.6 us -> none  [the longest x1 3.22 us: local(): jnp.transpose(result, (2, 3, 4, 0, 5, 1, 6))]
    slice x8 -> x0, local copies, waits for them, and re-layouts: 5.2 us -> none  [the longest x6 2.64 us: padded_2(): last = lax.slice_in_dim(x, length - width, length, axis=dim)]
  transfers between devices with their start and end apart: 16 -> 12, of which waited for: 6 -> 7; matrix products, arithmetic and copies ran while one was open for 10% -> 0% of each run, Pallas kernels for 0% -> 9%
where the time goes in v1:
time: 90.8 us; the launch traced here: 89.5 us
  starting transfers between devices  36.1 us (40%)
  Pallas kernels  36 us (40%)
  waiting for transfers between devices  11.2 us (12%)
  other arithmetic  3.57 us (4%)
  local copies, waits for them, and re-layouts  2.41 us (3%)
    ppermute x3, starting transfers between devices, off(): return lax.ppermute(x, 'gx', swaps(nx, 1, True))  19.3 us
    pallas_call x1, Pallas kernels, local(): call(analysis, [(3072, 128)], [SM, SM, SM] + [VM] * 10, [pltpu.VMEM((9 *...  13.6 us
    pallas_call x1, Pallas kernels, local(): call(forecast, [(3072, 128), (128, 128)], [SM, SM] + [VM] * 7, [pltpu.VME...  10.6 us
    ppermute x3, starting transfers between devices, gyb(): return lax.ppermute(x, 'gy', swaps(ny, 1, False))  8.92 us
    pallas_call x1, Pallas kernels, local(): call(weights, [(1024, 128), (1024, 128)], [SM, SM, SM] + [VM] * 5, [pltpu...  6.57 us
    ppermute x3, waiting for transfers between devices, gyb(): return lax.ppermute(x, 'gy', swaps(ny, 1, False))  4.7 us
    ppermute x3, starting transfers between devices, gya(): return lax.ppermute(x, 'gy', swaps(ny, 0, False))  4.69 us
    pallas_call x1, Pallas kernels, local(): call(relayout, [(3072, 128), (1152, 128), (1152, 128), (80, 128), (80, 12...  3.8 us
  transfers between devices with their start and end apart: 12, of which 7 were waited for; matrix products, arithmetic and copies ran while one was open for 0% of the time, Pallas kernels for 9%

profile of v1, /device:TPU:2, one launch (start us, length us, event | category | flops | bytes accessed | tf_op | source)
XLA Modules:
  0.0 89.5 jit_solution(11659985288046829736)
XLA Ops:
  0.0 0.7 convert_element_type.9
  0.7 0.1 pad.6.clone
  0.8 0.7 pad_add_fusion.s_ref
  1.4 1.4 %maximum_maximum_fusion.st_ref = f32[8,128]{1,0:T(8,128)} fusion(f32[2,128]{1,0:T(2,128)S(1)} %bitcast.16, f32[2,128]{1,0:T(2,128)} %bitcast.19, f32[2,128]{1,0:T(2,128)} %bitcast.20, f32[8]{0:T(128)S(1)} %pad.6.clone), kind=kLoop, calls=%fused_computation.1 | loop fusion | flops 3072 | bytes 7200 | tf_op jit(solution)/shard_map/concatenate | solution.py:442
  2.8 3.8 %shard_map.64 = (f32[3072,128]{1,0:T(8,128)}, f32[1152,128]{1,0:T(8,128)}, f32[1152,128]{1,0:T(8,128)}, f32[80,128]{1,0:T(8,128)}, f32[80,128]{1,0:T(8,128)}) custom-call(s32[4]{0:T(128)} %pad_add_fusion.s_ref, f32[3072,128]{1,0:T(8,128)} %bitcast.12, f32[8,128]{1,0:T(8,128)} %maximum_maximum_fusion.st_ref), custom_call_target="tpu_custom_call" | custom-call | tf_op jit(solution)/shard_map/pallas_call | solution.py:454
  6.6 7.9 %collective-permute-start.4 = (f32[1152,128]{1,0:T(8,128)}, f32[1152,128]{1,0:T(8,128)S(1)}, u32[]{:S(2)}, u32[]{:S(2)}) collective-permute-start(f32[1152,128]{1,0:T(8,128)} %get-tuple-element.23), channel_id=1, source_target_pairs={{8,16},{16,8},{24,32},{32,24},{40,48},{48,40},{56,64},{64,56},{72,... | collective-permute-start | bytes 1769480 | tf_op jit(solution)/shard_map/ppermute | solution.py:433
  14.5 0.0 collective-permute-start.5
  14.5 0.7 collective-permute-start
  15.2 3.2 %collective-permute-start.1 = (f32[80,128]{1,0:T(8,128)}, f32[80,128]{1,0:T(8,128)S(1)}, u32[]{:S(2)}, u32[]{:S(2)}) collective-permute-start(f32[80,128]{1,0:T(8,128)} %get-tuple-element.17), channel_id=1, source_target_pairs={{1,2},{2,1},{3,4},{4,3},{5,6},{6,5},{9,10},{10,9},{11,12},{12,11},... | collective-permute-start | bytes 122888 | tf_op jit(solution)/shard_map/ppermute | solution.py:439
  18.4 1.4 %collective-permute-done.ga_ref = f32[80,128]{1,0:T(8,128)S(1)} collective-permute-done((f32[80,128]{1,0:T(8,128)}, f32[80,128]{1,0:T(8,128)S(1)}, u32[]{:S(2)}, u32[]{:S(2)}) %collective-permute-start) | collective-permute-done | bytes 40992 | tf_op jit(solution)/shard_map/ppermute | solution.py:436
  19.8 0.0 copy-start.2
  19.8 2.3 %collective-permute-done.1.gb_ref = f32[80,128]{1,0:T(8,128)S(1)} collective-permute-done((f32[80,128]{1,0:T(8,128)}, f32[80,128]{1,0:T(8,128)S(1)}, u32[]{:S(2)}, u32[]{:S(2)}) %collective-permute-start.1) | collective-permute-done | bytes 40992 | tf_op jit(solution)/shard_map/ppermute | solution.py:439
  22.2 0.0 copy-done.2
  22.2 0.0 copy-start.3
  22.2 0.6 copy-done.3
  22.8 1.5 %shard_map.65 = (f32[80,128]{1,0:T(8,128)}, f32[80,128]{1,0:T(8,128)}) custom-call(s32[4]{0:T(128)} %pad_add_fusion.s_ref, f32[8,128]{1,0:T(8,128)} %maximum_maximum_fusion.st_ref, f32[80,128]{1,0:T(8,128)} %copy-done.2, f32[80,128]{1,0:T(8,128)} %copy-done.3), custom_call_target="tpu_custom_call" | custom-call | tf_op jit(solution)/shard_map/pallas_call | solution.py:463
  24.3 3.4 %collective-permute-start.2 = (f32[80,128]{1,0:T(8,128)}, f32[80,128]{1,0:T(8,128)S(1)}, u32[]{:S(2)}, u32[]{:S(2)}) collective-permute-start(f32[80,128]{1,0:T(8,128)} %get-tuple-element.18), channel_id=1, source_target_pairs={{8,16},{16,8},{24,32},{32,24},{40,48},{48,40},{56,64},{64,56},{72,... | collective-permute-start | bytes 122888 | tf_op jit(solution)/shard_map/ppermute | solution.py:433
  27.7 3.0 %collective-permute-start.3 = (f32[80,128]{1,0:T(8,128)}, f32[80,128]{1,0:T(8,128)S(1)}, u32[]{:S(2)}, u32[]{:S(2)}) collective-permute-start(f32[80,128]{1,0:T(8,128)} %get-tuple-element.19), channel_id=1, source_target_pairs={{0,8},{8,0},{16,24},{24,16},{32,40},{40,32},{48,56},{56,48},{64,72... | collective-permute-start | bytes 122888 | tf_op jit(solution)/shard_map/ppermute | solution.py:430
  30.7 0.8 collective-permute-done.2.coff_ref
  31.5 0.0 copy-start.7
  31.5 0.2 collective-permute-done.3.con_ref
  31.8 0.0 copy-start.8
  31.8 0.0 collective-permute-done.4.roff_ref
  31.8 0.0 copy-start
  31.8 0.0 collective-permute-done.5.ron_ref
  31.8 0.0 copy-start.1
  31.8 0.3 copy-done.7
  32.1 0.3 copy-done.8
  32.4 0.2 copy-done
  32.6 0.2 copy-done.1
  32.8 10.6 %shard_map.67 = (f32[3072,128]{1,0:T(8,128)}, f32[128,128]{1,0:T(8,128)}) custom-call(s32[4]{0:T(128)} %pad_add_fusion.s_ref, s32[256]{0:T(256)} %bitcast.15, f32[3072,128]{1,0:T(8,128)} %get-tuple-element.22.t_ref, f32[1152,128]{1,0:T(8,128)} %copy-done, f32[1152,128]{1,0:T(8,128)} %copy-done.1, f32[80,128]{1,0:T(8,128)} %copy-done.2, f32[80,128]{1,0:T(8,128)} %copy-done.3, ...), custom_call_target="tpu_custom_call" | custom-call | tf_op jit(solution)/shard_map/pallas_call | solution.py:467
  43.4 3.0 %collective-permute-start.7 = (f32[128,128]{1,0:T(8,128)}, f32[128,128]{1,0:T(8,128)S(1)}, u32[]{:S(2)}, u32[]{:S(2)}) collective-permute-start(f32[128,128]{1,0:T(8,128)} %get-tuple-element.25.own_ref), channel_id=1, source_target_pairs={{1,2},{2,1},{3,4},{4,3},{5,6},{6,5},{9,10},{10,9},{11,12},{12,11},... | collective-permute-start | bytes 196616 | tf_op jit(solution)/shard_map/ppermute | solution.py:439
  46.4 2.0 %collective-permute-start.6 = (f32[128,128]{1,0:T(8,128)}, f32[128,128]{1,0:T(8,128)S(1)}, u32[]{:S(2)}, u32[]{:S(2)}) collective-permute-start(f32[128,128]{1,0:T(8,128)} %get-tuple-element.25.own_ref), channel_id=1, source_target_pairs={{0,1},{1,0},{2,3},{3,2},{4,5},{5,4},{6,7},{7,6},{8,9},{9,8},{10,11... | collective-permute-start | bytes 196616 | tf_op jit(solution)/shard_map/ppermute | solution.py:436
  48.4 2.4 %collective-permute-done.7.ob_ref = f32[128,128]{1,0:T(8,128)S(1)} collective-permute-done((f32[128,128]{1,0:T(8,128)}, f32[128,128]{1,0:T(8,128)S(1)}, u32[]{:S(2)}, u32[]{:S(2)}) %collective-permute-start.7) | collective-permute-done | bytes 65568 | tf_op jit(solution)/shard_map/ppermute | solution.py:439
  50.7 0.0 copy-start.4
  50.7 1.8 %collective-permute-done.6.oa_ref = f32[128,128]{1,0:T(8,128)S(1)} collective-permute-done((f32[128,128]{1,0:T(8,128)}, f32[128,128]{1,0:T(8,128)S(1)}, u32[]{:S(2)}, u32[]{:S(2)}) %collective-permute-start.6) | collective-permute-done | bytes 65568 | tf_op jit(solution)/shard_map/ppermute | solution.py:436
  52.6 0.0 copy-start.5
  52.6 0.9 pad_maximum_fusion
  53.4 0.2 collective-permute-start.8
  53.6 7.9 %collective-permute-start.9 = (f32[128,128]{1,0:T(8,128)}, f32[128,128]{1,0:T(8,128)S(1)}, u32[]{:S(2)}, u32[]{:S(2)}) collective-permute-start(f32[128,128]{1,0:T(8,128)} %get-tuple-element.25.own_ref), channel_id=1, source_target_pairs={{8,16},{16,8},{24,32},{32,24},{40,48},{48,40},{56,64},{64,56},{72,... | collective-permute-start | bytes 196616 | tf_op jit(solution)/shard_map/ppermute | solution.py:433
  61.6 2.2 %collective-permute-done.9.off_ref = f32[128,128]{1,0:T(8,128)S(1)} collective-permute-done((f32[128,128]{1,0:T(8,128)}, f32[128,128]{1,0:T(8,128)S(1)}, u32[]{:S(2)}, u32[]{:S(2)}) %collective-permute-start.9) | collective-permute-done | bytes 65568 | tf_op jit(solution)/shard_map/ppermute | solution.py:433
  63.8 0.0 copy-start.9
  63.8 2.7 %collective-permute-start.11 = (f32[128,128]{1,0:T(8,128)S(1)}, f32[128,128]{1,0:T(8,128)S(1)}, u32[]{:S(2)}, u32[]{:S(2)}) collective-permute-start(f32[128,128]{1,0:T(8,128)S(1)} %collective-permute-done.9.off_ref), channel_id=1, source_target_pairs={{1,2},{2,1},{3,4},{4,3},{5,6},{6,5},{9,10},{10,9},{11,12},{12,11},... | collective-permute-start | bytes 196616 | tf_op jit(solution)/shard_map/ppermute | solution.py:439
  66.5 2.1 %collective-permute-start.10 = (f32[128,128]{1,0:T(8,128)S(1)}, f32[128,128]{1,0:T(8,128)S(1)}, u32[]{:S(2)}, u32[]{:S(2)}) collective-permute-start(f32[128,128]{1,0:T(8,128)S(1)} %collective-permute-done.9.off_ref), channel_id=1, source_target_pairs={{0,1},{1,0},{2,3},{3,2},{4,5},{5,4},{6,7},{7,6},{8,9},{9,8},{10,11... | collective-permute-start | bytes 196616 | tf_op jit(solution)/shard_map/ppermute | solution.py:436
  68.6 6.6 %shard_map.66 = (f32[1024,128]{1,0:T(8,128)}, f32[1024,128]{1,0:T(8,128)}) custom-call(s32[4]{0:T(128)} %pad_add_fusion.s_ref, s32[16]{0:T(128)} %bitcast.17, s32[2048]{0:T(1024)} %bitcast.13, f32[8,128]{1,0:T(8,128)} %maximum_maximum_fusion.st_ref, f32[80,128]{1,0:T(8,128)} %copy-done.2, f32[80,128]{1,0:T(8,128)} %copy-done.3, f32[80,128]{1,0:T(8,128)} %copy-done.7, ...), custom_call_target="tpu_custom_call" | custom-call | tf_op jit(solution)/shard_map/pallas_call | solution.py:473
  75.1 0.0 collective-permute-done.11.fb_ref
  75.1 0.0 copy-start.10
  75.2 0.0 collective-permute-done.10.fa_ref
  75.2 0.0 copy-start.11
  75.2 0.0 collective-permute-done.8.on_ref
  75.2 0.0 copy-start.6
  75.2 0.0 copy-done.4
  75.2 0.0 copy-done.5
  75.2 0.0 copy-done.9
  75.2 0.5 copy-done.10
  75.8 0.0 copy-done.11
  75.8 0.1 copy-done.6
  75.9 13.6 %shard_map.68 = f32[3072,128]{1,0:T(8,128)} custom-call(s32[4]{0:T(128)} %pad_add_fusion.s_ref, s32[16]{0:T(128)} %bitcast.18, s32[2048]{0:T(1024)} %bitcast.14, f32[1024,128]{1,0:T(8,128)} %get-tuple-element.20.r_ref, f32[1024,128]{1,0:T(8,128)} %get-tuple-element.21.v_ref, f32[128,128]{1,0:T(8,128)} %get-tuple-element.25.own_ref, f32[128,128]{1,0:T(8,128)} %copy-done.5, ...), custom_call_target="tpu_custom_call" | custom-call | tf_op jit(solution)/shard_map/pallas_call | solution.py:487
  (1 shorter events, 0.0 us)
Async XLA Ops:
  6.6 25.2 %collective-permute-start.4 = (f32[1152,128]{1,0:T(8,128)}, f32[1152,128]{1,0:T(8,128)S(1)}, u32[]{:S(2)}, u32[]{:S(2)}) collective-permute-start(f32[1152,128]{1,0:T(8,128)} %get-tuple-element.23), channel_id=1, source_target_pairs={{8,16},{16,8},{24,32},{32,24},{40,48},{48,40},{56,64},{64,56},{72,... | collective-permute-start | bytes 1769480 | tf_op jit(solution)/shard_map/ppermute | solution.py:433
  14.5 17.3 %collective-permute-start.5 = (f32[1152,128]{1,0:T(8,128)}, f32[1152,128]{1,0:T(8,128)S(1)}, u32[]{:S(2)}, u32[]{:S(2)}) collective-permute-start(f32[1152,128]{1,0:T(8,128)} %get-tuple-element.24), channel_id=1, source_target_pairs={{0,8},{8,0},{16,24},{24,16},{32,40},{40,32},{48,56},{56,48},{64,72... | collective-permute-start | bytes 1769480 | tf_op jit(solution)/shard_map/ppermute | solution.py:430
  14.5 5.3 %collective-permute-start = (f32[80,128]{1,0:T(8,128)}, f32[80,128]{1,0:T(8,128)S(1)}, u32[]{:S(2)}, u32[]{:S(2)}) collective-permute-start(f32[80,128]{1,0:T(8,128)} %get-tuple-element.16), channel_id=1, source_target_pairs={{0,1},{1,0},{2,3},{3,2},{4,5},{5,4},{6,7},{7,6},{8,9},{9,8},{10,11... | collective-permute-start | bytes 122888 | tf_op jit(solution)/shard_map/ppermute | solution.py:436
  15.2 7.0 %collective-permute-start.1 = (f32[80,128]{1,0:T(8,128)}, f32[80,128]{1,0:T(8,128)S(1)}, u32[]{:S(2)}, u32[]{:S(2)}) collective-permute-start(f32[80,128]{1,0:T(8,128)} %get-tuple-element.17), channel_id=1, source_target_pairs={{1,2},{2,1},{3,4},{4,3},{5,6},{6,5},{9,10},{10,9},{11,12},{12,11},... | collective-permute-start | bytes 122888 | tf_op jit(solution)/shard_map/ppermute | solution.py:439
  19.8 2.4 %copy-start.2 = (f32[80,128]{1,0:T(8,128)}, f32[80,128]{1,0:T(8,128)S(1)}, u32[]{:S(2)}) copy-start(f32[80,128]{1,0:T(8,128)S(1)} %collective-permute-done.ga_ref) | copy-start | bytes 122884
  22.2 0.6 copy-start.3
  24.3 7.3 %collective-permute-start.2 = (f32[80,128]{1,0:T(8,128)}, f32[80,128]{1,0:T(8,128)S(1)}, u32[]{:S(2)}, u32[]{:S(2)}) collective-permute-start(f32[80,128]{1,0:T(8,128)} %get-tuple-element.18), channel_id=1, source_target_pairs={{8,16},{16,8},{24,32},{32,24},{40,48},{48,40},{56,64},{64,56},{72,... | collective-permute-start | bytes 122888 | tf_op jit(solution)/shard_map/ppermute | solution.py:433
  27.7 4.1 %collective-permute-start.3 = (f32[80,128]{1,0:T(8,128)}, f32[80,128]{1,0:T(8,128)S(1)}, u32[]{:S(2)}, u32[]{:S(2)}) collective-permute-start(f32[80,128]{1,0:T(8,128)} %get-tuple-element.19), channel_id=1, source_target_pairs={{0,8},{8,0},{16,24},{24,16},{32,40},{40,32},{48,56},{56,48},{64,72... | collective-permute-start | bytes 122888 | tf_op jit(solution)/shard_map/ppermute | solution.py:430
  31.5 0.6 copy-start.7
  31.8 0.6 copy-start.8
  31.8 0.8 copy-start
  31.8 1.0 %copy-start.1 = (f32[1152,128]{1,0:T(8,128)}, f32[1152,128]{1,0:T(8,128)S(1)}, u32[]{:S(2)}) copy-start(f32[1152,128]{1,0:T(8,128)S(1)} %collective-permute-done.5.ron_ref) | copy-start | bytes 1769476
  43.4 7.3 %collective-permute-start.7 = (f32[128,128]{1,0:T(8,128)}, f32[128,128]{1,0:T(8,128)S(1)}, u32[]{:S(2)}, u32[]{:S(2)}) collective-permute-start(f32[128,128]{1,0:T(8,128)} %get-tuple-element.25.own_ref), channel_id=1, source_target_pairs={{1,2},{2,1},{3,4},{4,3},{5,6},{6,5},{9,10},{10,9},{11,12},{12,11},... | collective-permute-start | bytes 196616 | tf_op jit(solution)/shard_map/ppermute | solution.py:439
  46.4 6.1 %collective-permute-start.6 = (f32[128,128]{1,0:T(8,128)}, f32[128,128]{1,0:T(8,128)S(1)}, u32[]{:S(2)}, u32[]{:S(2)}) collective-permute-start(f32[128,128]{1,0:T(8,128)} %get-tuple-element.25.own_ref), channel_id=1, source_target_pairs={{0,1},{1,0},{2,3},{3,2},{4,5},{5,4},{6,7},{7,6},{8,9},{9,8},{10,11... | collective-permute-start | bytes 196616 | tf_op jit(solution)/shard_map/ppermute | solution.py:436
  50.7 24.5 %copy-start.4 = (f32[128,128]{1,0:T(8,128)}, f32[128,128]{1,0:T(8,128)S(1)}, u32[]{:S(2)}) copy-start(f32[128,128]{1,0:T(8,128)S(1)} %collective-permute-done.7.ob_ref) | copy-start | bytes 196612
  52.6 22.7 %copy-start.5 = (f32[128,128]{1,0:T(8,128)}, f32[128,128]{1,0:T(8,128)S(1)}, u32[]{:S(2)}) copy-start(f32[128,128]{1,0:T(8,128)S(1)} %collective-permute-done.6.oa_ref) | copy-start | bytes 196612
  53.4 21.7 %collective-permute-start.8 = (f32[384,128]{1,0:T(8,128)S(1)}, f32[384,128]{1,0:T(8,128)S(1)}, u32[]{:S(2)}, u32[]{:S(2)}) collective-permute-start(f32[384,128]{1,0:T(8,128)S(1)} %pad_maximum_fusion), channel_id=1, source_target_pairs={{0,8},{8,0},{16,24},{24,16},{32,40},{40,32},{48,56},{56,48},{64,72... | collective-permute-start | bytes 589832 | tf_op jit(solution)/shard_map/ppermute | solution.py:430
  53.6 10.1 %collective-permute-start.9 = (f32[128,128]{1,0:T(8,128)}, f32[128,128]{1,0:T(8,128)S(1)}, u32[]{:S(2)}, u32[]{:S(2)}) collective-permute-start(f32[128,128]{1,0:T(8,128)} %get-tuple-element.25.own_ref), channel_id=1, source_target_pairs={{8,16},{16,8},{24,32},{32,24},{40,48},{48,40},{56,64},{64,56},{72,... | collective-permute-start | bytes 196616 | tf_op jit(solution)/shard_map/ppermute | solution.py:433
  63.8 11.4 %copy-start.9 = (f32[128,128]{1,0:T(8,128)}, f32[128,128]{1,0:T(8,128)S(1)}, u32[]{:S(2)}) copy-start(f32[128,128]{1,0:T(8,128)S(1)} %collective-permute-done.9.off_ref) | copy-start | bytes 196612
  63.8 11.4 %collective-permute-start.11 = (f32[128,128]{1,0:T(8,128)S(1)}, f32[128,128]{1,0:T(8,128)S(1)}, u32[]{:S(2)}, u32[]{:S(2)}) collective-permute-start(f32[128,128]{1,0:T(8,128)S(1)} %collective-permute-done.9.off_ref), channel_id=1, source_target_pairs={{1,2},{2,1},{3,4},{4,3},{5,6},{6,5},{9,10},{10,9},{11,12},{12,11},... | collective-permute-start | bytes 196616 | tf_op jit(solution)/shard_map/ppermute | solution.py:439
  66.5 8.6 %collective-permute-start.10 = (f32[128,128]{1,0:T(8,128)S(1)}, f32[128,128]{1,0:T(8,128)S(1)}, u32[]{:S(2)}, u32[]{:S(2)}) collective-permute-start(f32[128,128]{1,0:T(8,128)S(1)} %collective-permute-done.9.off_ref), channel_id=1, source_target_pairs={{0,1},{1,0},{2,3},{3,2},{4,5},{5,4},{6,7},{7,6},{8,9},{9,8},{10,11... | collective-permute-start | bytes 196616 | tf_op jit(solution)/shard_map/ppermute | solution.py:436
  75.1 0.6 copy-start.10
  75.2 0.6 copy-start.11
  75.2 0.7 copy-start.6
